TPU v7x, 512 devices: a whole 4x4x16 slice. The times are simulated.
512 devices in a mesh: dom: 64 (over y, z_lo, core), cls: 8 (over z_hi, x).
Axes of the slice: x: 4, y: 4, z: 16 (z_hi: 2, z_lo: 8; z = z_hi * 8 + z_lo), core: 2. Of those that a mesh axis runs over, the one named last changes fastest.
Arguments:
- particles: bfloat16 [36864, 4096], P('dom'), may hold values from -6 to 6
- shift_index: int32 [36864], P('dom'), may hold values from 0 to 24
- prev_class: int32 [36864], P('dom'), may hold values from 0 to 63
- prev_rotation: int32 [36864], P('dom'), may hold values from 0 to 23
- precision: float32 [36864], P('dom'), may hold values from 0.25 to 300
- references: bfloat16 [64, 98304], P('cls', 'dom')
Outputs:
- new_references: float32 [64, 98304], P('cls', 'dom')
- log_evidence: float32 [36864], P('dom')
All inputs are finite; a program needn't handle non-finite values.
Results may differ from a plain program's by a relative error of at most 0.0039.
Values may be sent and summed in bfloat16 or wider, within the bound.
No kernel may reach another device: no remote copies, remote signals or barrier semaphores. Data moves between devices by JAX's collectives and lax.ppermute only.
A program may use at most 64 MiB of HBM per device.

v0:
```python
import math
import jax
import jax.numpy as jnp
from jax import lax
from jax.sharding import PartitionSpec as P

BOX = 64
F = 4096
R = 24
two_pi = 2.0 * math.pi
shift_side = 5
class_reward = 1.0
prior_mass = 1.0


def shift_particles(particles, shift_index, box_side):
    half_width = particles.shape[1] // 2
    frequency = jnp.arange(half_width, dtype=jnp.int32)
    freq_x = frequency % box_side - box_side // 2
    freq_y = frequency // box_side
    step_x = shift_index % shift_side - 2
    step_y = shift_index // shift_side - 2
    phase_int = (freq_x[None, :] * step_x[:, None] + freq_y[None, :] * step_y[:, None]) % box_side
    phase_angle = phase_int.astype(jnp.float32) * (two_pi / box_side)
    cosine_values = jnp.cos(phase_angle)
    sine_values = jnp.sin(phase_angle)
    real_part = particles[:, :half_width].astype(jnp.float32)
    imag_part = particles[:, half_width:].astype(jnp.float32)
    out_real = real_part * cosine_values + imag_part * sine_values
    out_imag = imag_part * cosine_values - real_part * sine_values
    return jnp.concatenate([out_real, out_imag], axis=1).astype(jnp.bfloat16)


def prior_term(prev_class, prev_rotation, class_ids, rotation_ids, rotations):
    rotation_distance = jnp.abs(rotation_ids[None, :] - prev_rotation[:, None])
    rotation_distance = jnp.minimum(rotation_distance, rotations - rotation_distance).astype(
        jnp.float32
    )
    prior_spread_width = rotations / 8.0
    match_flags = (class_ids[None, :] == prev_class[:, None]).astype(jnp.float32)
    return (
        -rotation_distance * rotation_distance / (2.0 * prior_spread_width * prior_spread_width)
        + class_reward * match_flags
    )


def on_device(particles, shift_index, prev_class, prev_rotation, precision, references):
    local_classes = references.shape[0]
    columns = references.shape[1]
    gathered = lax.all_gather(references, "dom", axis=1, tiled=True)
    table = gathered.reshape(local_classes * R, F)
    half_norm = 0.5 * jnp.sum(jnp.square(table.astype(jnp.float32)), axis=1)
    candidate = jnp.arange(local_classes * R, dtype=jnp.int32)
    class_ids = lax.axis_index("cls") * local_classes + candidate // R
    rotation_ids = candidate % R
    shifted = shift_particles(particles, shift_index, BOX)
    correlation = lax.dot_general(
        shifted, table, (((1,), (1,)), ((), ())), preferred_element_type=jnp.float32
    )
    scores = precision[:, None] * (correlation - half_norm[None, :])
    scores = scores + prior_term(prev_class, prev_rotation, class_ids, rotation_ids, R)
    local_top = jnp.max(scores, axis=1)
    top_score = lax.pmax(local_top, "cls")
    exponent = jnp.exp(scores - top_score[:, None])
    total_mass = lax.psum(jnp.sum(exponent, axis=1), "cls")
    probs = exponent / total_mass[:, None]
    weights = probs.astype(jnp.bfloat16)
    numerator = lax.dot_general(
        weights, shifted, (((0,), (0,)), ((), ())), preferred_element_type=jnp.float32
    )
    numerator = numerator.reshape(local_classes, R * F)
    occupancy = jnp.sum(probs, axis=0).reshape(local_classes, R)
    start = lax.axis_index("dom") * columns
    summed, occupancy = lax.psum((numerator, occupancy), "dom")
    mine = lax.dynamic_slice_in_dim(summed, start, columns, 1)
    spread = jnp.broadcast_to(occupancy[:, :, None], (local_classes, R, F)).reshape(
        local_classes, R * F
    )
    mass_columns = lax.dynamic_slice_in_dim(spread, start, columns, 1)
    refreshed_references = mine / (mass_columns + prior_mass)
    evidence = top_score + jnp.log(total_mass)
    return (refreshed_references, evidence)


def solution(mesh):
    return jax.shard_map(
        on_device,
        mesh=mesh,
        in_specs=(P("dom", None), P("dom"), P("dom"), P("dom"), P("dom"), P("cls", "dom")),
        out_specs=(P("cls", "dom"), P("dom")),
        check_vma=False,
    )
```

profile of v0, /device:TPU:1, one launch (start us, length us, event | category | flops | bytes accessed | tf_op | source)
XLA Modules:
  0.0 1063.9 jit_solution(16293794462568525287)
XLA Ops:
  7.2 0.0 all-gather.2.cloned.1.call-start
  7.2 0.7 all-gather.2.cloned.1.call-update
  7.9 0.0 all-reduce.2.cloned.1.call-start
  8.0 0.7 fusion.28
  8.7 23.3 %fusion.1 = (bf16[576,2048]{1,0:T(8,128)(2,1)}, bf16[576,2048]{1,0:T(8,128)(2,1)}) fusion(s32[576]{0:T(1024)S(1)} %get-tuple-element.5, s32[2048]{0:T(1024)S(1)} %get-tuple-element.8, s32[576]{0:T(1024)S(1)} %get-tuple-element.4, s32[2048]{0:T(1024)S(1)} %get-tuple-element.9, bf16[576,4096]{1,0:T(8,128)(2,1)} %param.6), kind=kLoop, calls=%fused_computation.8 | loop fusion | flops 30670848 | bytes 9458176 | tf_op jit(solution)/shard_map/convert
  32.0 0.0 copy-start.1
  32.0 0.0 copy-start.2
  32.0 0.0 copy-start.3
  32.0 104.3 %all-gather.2.cloned.1.call-done = bf16[8,98304]{1,0:T(8,128)(2,1)} async-done(((bf16[8,1536]{1,0:T(8,128)(2,1)}), bf16[8,98304]{1,0:T(8,128)(2,1)}) %all-gather.2.cloned.1.call-update) | async-done | bytes 1572880 | tf_op jit(solution)/shard_map/all_gather | solution.py:50
  136.3 2.1 reshape.71
  138.4 0.4 multiply_reduce_fusion
  138.8 0.0 copy-done.1
  138.8 0.0 copy-done.2
  138.8 0.0 copy-done.3
  138.8 4.3 fusion.35
  143.1 0.0 copy-start
  143.1 38.3 %pmax.7 = f32[576]{0:T(1024)S(1)} all-reduce(f32[576]{0:T(1024)S(1)} %get-tuple-element.6), channel_id=1, replica_groups=mesh['dom'=64,'cls'=8] {'cls'}, use_global_device_ids=true, to_apply=%region_2.3 | all-reduce | flops 576 | bytes 4608 | tf_op jit(solution)/shard_map/pmax | solution.py:63
  181.5 0.1 fusion.18
  181.6 0.0 copy-done
  181.6 29.9 %psum.21 = f32[576]{0:T(1024)S(1)} all-reduce(f32[576]{0:T(1024)S(1)} %fusion.18), channel_id=1, replica_groups=mesh['dom'=64,'cls'=8] {'cls'}, use_global_device_ids=true, to_apply=%region_4.5 | all-reduce | flops 576 | bytes 4608 | tf_op jit(solution)/shard_map/psum | solution.py:65
  211.5 3.9 fusion.7
  215.5 2.3 reshape.72
  217.7 0.0 all-reduce.2.cloned.1.call-update
  217.7 1.2 fusion.20
  218.9 0.1 reshape.73
  219.0 217.7 %psum.23 = f32[8,24]{1,0:T(8,128)S(1)} all-reduce(f32[8,24]{1,0:T(8,128)S(1)} %reshape.73), channel_id=1, replica_groups=mesh['dom'=64,'cls'=8] {'dom'}, use_global_device_ids=true, to_apply=%region_7.8 | all-reduce | flops 192 | bytes 1536 | tf_op jit(solution)/shard_map/psum | solution.py:74
  436.7 0.1 copy.8
  436.8 0.6 log_add_fusion
  437.4 618.0 %all-reduce.2.cloned.1.call-done = f32[8,98304]{1,0:T(8,128)} async-done(((f32[8,98304]{1,0:T(8,128)}), f32[8,98304]{1,0:T(8,128)}) %all-reduce.2.cloned.1.call-update) | async-done | bytes 3145744 | tf_op jit(solution)/shard_map/psum | solution.py:74
  1055.3 0.3 broadcast_in_dim.2
  1055.6 1.4 add_divide_fusion
  (3 shorter events, 0.0 us)
Async XLA Ops:
  7.2 129.1 %all-gather.2.cloned.1.call-start = ((), (), s32[]{:S(2)}) async-start(), calls=%async_computation | async-start | bytes 1597440 | tf_op jit(solution)/shard_map/all_gather | solution.py:50
  7.9 1047.4 %all-reduce.2.cloned.1.call-start = ((), (), s32[]{:S(2)}) async-start(), calls=%async_computation.1 | async-start | bytes 6291456 | tf_op jit(solution)/shard_map/psum | solution.py:74
  32.0 106.8 %copy-start.1 = (s32[576]{0:T(1024)S(1)}, s32[576]{0:T(1024)}, u32[]{:S(2)}) copy-start(s32[576]{0:T(1024)} %param.8) | copy-start | bytes 6916
  32.0 106.8 %copy-start.2 = (s32[576]{0:T(1024)S(1)}, s32[576]{0:T(1024)}, u32[]{:S(2)}) copy-start(s32[576]{0:T(1024)} %param.9) | copy-start | bytes 6916
  32.0 106.8 %copy-start.3 = (f32[576]{0:T(1024)S(1)}, f32[576]{0:T(1024)}, u32[]{:S(2)}) copy-start(f32[576]{0:T(1024)} %param.10) | copy-start | bytes 6916
  143.1 38.4 %copy-start = (f32[576,192]{0,1:T(8,128)}, f32[576,192]{0,1:T(8,128)S(1)}, u32[]{:S(2)}) copy-start(f32[576,192]{0,1:T(8,128)S(1)} %get-tuple-element.7) | copy-start | bytes 1327108
Sparse Core Ops, SparseCore 0:
  10.1 126.0 all-gather.1
  217.9 837.4 all-reduce.1
where the time goes:
time: 1060 us
  waiting for transfers between devices  723 us (68%)
  blocking collectives  286 us (27%)
  other arithmetic  27.7 us (3%)
  between operations  14.1 us (1%)
    psum x1, waiting for transfers between devices, on_device(): summed, occupancy = lax.psum((numerator, occupancy), 'dom')  618 us
    psum x1, blocking collectives, on_device(): summed, occupancy = lax.psum((numerator, occupancy), 'dom')  218 us
    all_gather x1, waiting for transfers between devices, on_device(): gathered = lax.all_gather(references, 'dom', axis=1, tiled=True)  104 us
    pmax x1, blocking collectives, on_device(): top_score = lax.pmax(local_top, 'cls')  38.3 us
    psum x1, blocking collectives, on_device(): total_mass = lax.psum(jnp.sum(exponent, axis=1), 'cls')  29.9 us
    another operation x1, other arithmetic  23.3 us
  transfers between devices with their start and end apart: 2, of which 2 were waited for; matrix products, arithmetic and copies ran while one was open for 2% of the time, Pallas kernels for 0%

commit v1 on v0

--- a/solution.py
+++ b/solution.py
@@ -47,7 +47,12 @@
 def on_device(particles, shift_index, prev_class, prev_rotation, precision, references):
     local_classes = references.shape[0]
     columns = references.shape[1]
-    gathered = lax.all_gather(references, "dom", axis=1, tiled=True)
+    gathered = jnp.concatenate(
+        lax.all_to_all(
+            jnp.stack([references for _ in range(lax.psum(1, "dom"))], axis=0), "dom", 0, 0
+        ),
+        axis=1,
+    )
     table = gathered.reshape(local_classes * R, F)
     half_norm = 0.5 * jnp.sum(jnp.square(table.astype(jnp.float32)), axis=1)
     candidate = jnp.arange(local_classes * R, dtype=jnp.int32)

time: 1060 us -> 1030 us (0.972)
  waiting for transfers between devices: 723 us -> 670 us
  starting transfers between devices: 0.08 us -> 17.3 us
    all_gather x1 -> x0, waiting for transfers between devices: 104 us -> none  [on_device(): gathered = lax.all_gather(references, 'dom', axis=1, tiled=True)]
    all_to_all x0 -> x1, waiting for transfers between devices: none -> 50.1 us  [on_device(): lax.all_to_all(jnp.stack([references for _ in range(lax.psum(1, 'dom'))],...]
    all_to_all x0 -> x1, starting transfers between devices: none -> 17.2 us  [on_device(): lax.all_to_all(jnp.stack([references for _ in range(lax.psum(1, 'dom'))],...]
where the time goes in v1:
time: 1030 us
  waiting for transfers between devices  670 us (65%)
  blocking collectives  285 us (28%)
  other arithmetic  27.1 us (3%)
  starting transfers between devices  17.3 us (2%)
  between operations  14.2 us (1%)
    psum x1, waiting for transfers between devices, on_device(): summed, occupancy = lax.psum((numerator, occupancy), 'dom')  620 us
    psum x1, blocking collectives, on_device(): summed, occupancy = lax.psum((numerator, occupancy), 'dom')  217 us
    all_to_all x1, waiting for transfers between devices, on_device(): lax.all_to_all(jnp.stack([references for _ in range(lax.psum(1, 'dom'))],...  50.1 us
    pmax x1, blocking collectives, on_device(): top_score = lax.pmax(local_top, 'cls')  38.1 us
    psum x1, blocking collectives, on_device(): total_mass = lax.psum(jnp.sum(exponent, axis=1), 'cls')  29.9 us
    another operation x1, other arithmetic  23.3 us
  transfers between devices with their start and end apart: 2, of which 2 were waited for; matrix products, arithmetic and copies ran while one was open for 2% of the time, Pallas kernels for 0%

profile of v1, /device:TPU:1, one launch (start us, length us, event | category | flops | bytes accessed | tf_op | source)
XLA Modules:
  0.0 1029.1 jit_solution(6891757854963655140)
XLA Ops:
  7.2 0.0 copy-start.1
  7.2 2.0 stack.2
  9.2 17.2 %all-to-all-start = ((bf16[64,8,1536]{2,1,0:T(8,128)(2,1)}), bf16[64,8,1536]{2,1,0:T(8,128)(2,1)S(1)}, u32[]{:S(2)}, u32[]{:S(2)}) async-start(bf16[64,8,1536]{2,1,0:T(8,128)(2,1)} %stack.2), calls=%async_computation | async-start | bytes 3145728 | tf_op jit(solution)/shard_map/all_to_all | solution.py:51
  26.4 0.0 all-reduce.2.cloned.1.call-start
  26.5 0.0 copy-done.1
  26.5 23.3 %fusion.1 = (bf16[576,2048]{1,0:T(8,128)(2,1)}, bf16[576,2048]{1,0:T(8,128)(2,1)}) fusion(s32[576]{0:T(1024)S(1)} %get-tuple-element.5, s32[2048]{0:T(1024)S(1)} %get-tuple-element.8, s32[576]{0:T(1024)S(1)} %get-tuple-element.4, s32[2048]{0:T(1024)S(1)} %get-tuple-element.9, bf16[576,4096]{1,0:T(8,128)(2,1)} %param.6), kind=kLoop, calls=%fused_computation.8 | loop fusion | flops 30670848 | bytes 9458176 | tf_op jit(solution)/shard_map/convert
  49.8 0.0 copy-start.2
  49.8 0.0 copy-start.3
  49.8 0.0 copy-start.4
  49.8 50.1 %all-to-all-done = bf16[64,8,1536]{2,1,0:T(8,128)(2,1)S(1)} async-done(((bf16[64,8,1536]{2,1,0:T(8,128)(2,1)}), bf16[64,8,1536]{2,1,0:T(8,128)(2,1)S(1)}, u32[]{:S(2)}, u32[]{:S(2)}) %all-to-all-start) | async-done | bytes 1572896 | tf_op jit(solution)/shard_map/all_to_all | solution.py:51
  99.9 0.5 copy.9
  100.4 1.9 reshape_reshape.3
  102.3 0.4 multiply_reduce_fusion
  102.7 0.0 copy-done.2
  102.7 0.0 copy-done.3
  102.7 0.0 copy-done.4
  102.7 4.3 fusion.35
  107.0 0.0 copy-start
  107.0 38.1 %pmax.7 = f32[576]{0:T(1024)S(1)} all-reduce(f32[576]{0:T(1024)S(1)} %get-tuple-element.6), channel_id=1, replica_groups=mesh['dom'=64,'cls'=8] {'cls'}, use_global_device_ids=true, to_apply=%region_2.3 | all-reduce | flops 576 | bytes 4608 | tf_op jit(solution)/shard_map/pmax | solution.py:68
  145.2 0.1 fusion.18
  145.3 0.0 copy-done
  145.3 29.9 %psum.21 = f32[576]{0:T(1024)S(1)} all-reduce(f32[576]{0:T(1024)S(1)} %fusion.18), channel_id=1, replica_groups=mesh['dom'=64,'cls'=8] {'cls'}, use_global_device_ids=true, to_apply=%region_4.5 | all-reduce | flops 576 | bytes 4608 | tf_op jit(solution)/shard_map/psum | solution.py:70
  175.2 3.9 fusion.7
  179.1 2.3 reshape.74
  181.4 0.0 all-reduce.2.cloned.1.call-update
  181.4 1.2 fusion.20
  182.6 0.1 reshape.75
  182.7 216.9 %psum.23 = f32[8,24]{1,0:T(8,128)S(1)} all-reduce(f32[8,24]{1,0:T(8,128)S(1)} %reshape.75), channel_id=1, replica_groups=mesh['dom'=64,'cls'=8] {'dom'}, use_global_device_ids=true, to_apply=%region_7.8 | all-reduce | flops 192 | bytes 1536 | tf_op jit(solution)/shard_map/psum | solution.py:79
  399.6 0.1 copy.10
  399.6 0.6 log_add_fusion
  400.2 620.2 %all-reduce.2.cloned.1.call-done = f32[8,98304]{1,0:T(8,128)} async-done(((f32[8,98304]{1,0:T(8,128)}), f32[8,98304]{1,0:T(8,128)}) %all-reduce.2.cloned.1.call-update) | async-done | bytes 3145744 | tf_op jit(solution)/shard_map/psum | solution.py:79
  1020.5 0.3 broadcast_in_dim.2
  1020.8 1.4 add_divide_fusion
  (4 shorter events, 0.0 us)
Async XLA Ops:
  7.2 19.3 %copy-start.1 = (s32[576]{0:T(1024)S(1)}, s32[576]{0:T(1024)}, u32[]{:S(2)}) copy-start(s32[576]{0:T(1024)} %param.7) | copy-start | bytes 6916
  9.2 90.7 %all-to-all-start = ((bf16[64,8,1536]{2,1,0:T(8,128)(2,1)}), bf16[64,8,1536]{2,1,0:T(8,128)(2,1)S(1)}, u32[]{:S(2)}, u32[]{:S(2)}) async-start(bf16[64,8,1536]{2,1,0:T(8,128)(2,1)} %stack.2), calls=%async_computation | async-start | bytes 3145728 | tf_op jit(solution)/shard_map/all_to_all | solution.py:51
  26.4 994.1 %all-reduce.2.cloned.1.call-start = ((), (), s32[]{:S(2)}) async-start(), calls=%async_computation.1 | async-start | bytes 6291456 | tf_op jit(solution)/shard_map/psum | solution.py:79
  49.8 52.9 %copy-start.2 = (s32[576]{0:T(1024)S(1)}, s32[576]{0:T(1024)}, u32[]{:S(2)}) copy-start(s32[576]{0:T(1024)} %param.8) | copy-start | bytes 6916
  49.8 52.9 %copy-start.3 = (s32[576]{0:T(1024)S(1)}, s32[576]{0:T(1024)}, u32[]{:S(2)}) copy-start(s32[576]{0:T(1024)} %param.9) | copy-start | bytes 6916
  49.8 52.9 %copy-start.4 = (f32[576]{0:T(1024)S(1)}, f32[576]{0:T(1024)}, u32[]{:S(2)}) copy-start(f32[576]{0:T(1024)} %param.10) | copy-start | bytes 6916
  107.0 38.2 %copy-start = (f32[576,192]{0,1:T(8,128)}, f32[576,192]{0,1:T(8,128)S(1)}, u32[]{:S(2)}) copy-start(f32[576,192]{0,1:T(8,128)S(1)} %get-tuple-element.7) | copy-start | bytes 1327108
Sparse Core Ops, SparseCore 0:
  181.5 838.9 all-reduce.1
